TPU v7x, 512 devices: a whole 4x8x8 slice. The times are simulated.
512 devices in a mesh: sat: 16 (over z, core), seg: 32 (over y, x).
Axes of the slice: x: 4, y: 8, z: 8, core: 2. Of those that a mesh axis runs over, the one named last changes fastest.
Arguments:
- sens_params: bfloat16 [16, 32, 320, 1024], P('sat', 'seg'), may hold values from -0.59765625 to 0.59765625
- sens_state: bfloat16 [16, 32, 320, 64], P('sat', 'seg'), may hold values from -0.59765625 to 0.59765625
- misfit: float32 [16, 32, 320], P('sat', 'seg'), may hold values from -6 to 6
- depth: float32 [16, 32, 320], P('sat', 'seg'), may hold values from 0.2 to 0.9
- cycle_count: int32 [16, 32], P('sat', 'seg'), may hold values from 80 to 320, as said below
- node_side: int32 [16, 32, 320], P('sat', 'seg'), may hold values from 0 to 1, as said below
- transition: bfloat16 [16, 32, 64, 64], P('sat', 'seg'), may hold values from -0.75 to 0.75
- cont_sens: bfloat16 [16, 32, 64, 1024], P('sat', 'seg'), may hold values from -0.59765625 to 0.59765625
- noise_root: float32 [16, 32, 64, 64], P('sat', 'seg'), may hold values from -0.4 to 0.4
- cont_misfit: float32 [16, 32, 64], P('sat', 'seg'), may hold values from -6 to 6
Outputs:
- gram_params: float32 [1024, 1024], P('sat')
- grad_params: float32 [1024], replicated
- node_hess: float32 [16, 32, 64, 64], P('sat', 'seg')
- node_cross: float32 [16, 32, 64, 1024], P('sat', 'seg')
- node_grad: float32 [16, 32, 64], P('sat', 'seg')
- node_coupling: float32 [16, 32, 64, 64], P('sat', 'seg')
Inputs may be any that keep to these rules, and one draw needn't show every extreme that they name: `cycle_count`: in every segment some satellite has exactly 320 cycles. `node_side`: along the cycles of one satellite's segment the value never falls, and both values occur.
All inputs are finite; a program needn't handle non-finite values.
Results may differ from a plain program's by a relative error of at most 0.0015.
The roundings to bfloat16 on the way count: a program that leaves them out, or rounds other values in their place, can miss the bound.
Values sent between devices are 32-bit elements; how exact they have to be, the bound alone decides.
A program may use at most 64 MiB of HBM per device.

v0:
```python
import jax
import jax.numpy as jnp
from jax import lax
from jax.sharding import PartitionSpec as P

highest = lax.Precision.HIGHEST


def entering(value, axis, combine, identity):
    devices, position = (lax.axis_size(axis), lax.axis_index(axis))
    everything = lax.all_gather(value, axis)
    start = jnp.broadcast_to(jnp.asarray(identity, value.dtype), value.shape)

    def step(k, before):
        reached = k < position
        new = combine(before, everything[k])
        return jnp.where(reached, new, before)

    return lax.fori_loop(0, devices, step, start)


def passed_along(block, axis, distance):
    devices = range(lax.axis_size(axis))
    route = [(i - distance, i) for i in devices if i - distance in devices]
    return lax.ppermute(block, axis, route)


def add_pair(earlier, later):
    return earlier + later


def shards(
    sens_params,
    sens_state,
    misfit,
    depth,
    cycle_count,
    node_side,
    transition,
    cont_sens,
    noise_root,
    cont_misfit,
):
    sat_dev = sens_params.shape[0]
    cycles = sens_params.shape[2]
    params = sens_params.shape[3]
    states = sens_state.shape[3]
    sat_count = lax.axis_size("sat")
    seg_count = lax.axis_size("seg")
    seg_place = lax.axis_index("seg")
    positions = jnp.arange(cycles, dtype=jnp.int32)
    live_mask = (positions[None, :] < cycle_count).astype(jnp.float32)
    used_depth = live_mask * depth[:, 0]
    through = jnp.sum(used_depth, axis=1)
    prior_age = entering(through, "seg", add_pair, jnp.zeros_like(through))
    upper_tri = (positions[:, None] < positions[None, :]).astype(jnp.float32)
    inner_age = jnp.dot(used_depth, upper_tri, precision=highest)
    age_scale = 4.0 / (cycles * seg_count)
    weights = live_mask / (1.0 + (prior_age[:, None] + inner_age) * age_scale)
    root_seg = jnp.sqrt(weights)
    weighted_sens = (root_seg[:, :, None] * sens_params[:, 0]).astype(jnp.bfloat16)
    weighted_res = (root_seg * misfit[:, 0]).astype(jnp.bfloat16)
    side = node_side[:, 0].astype(jnp.float32)[:, :, None]
    state_rows = root_seg[:, :, None] * sens_state[:, 0]
    state_pair = jnp.concatenate([state_rows * (1.0 - side), state_rows * side], axis=2).astype(
        jnp.bfloat16
    )
    live_link = (seg_place < seg_count - 1).astype(jnp.float32)
    eye_block = jnp.eye(states, dtype=jnp.float32)
    root_info = (eye_block[None] + noise_root[:, 0]) * live_link
    state_map = jnp.einsum(
        "sab,sbc->sac", root_info, transition[:, 0].astype(jnp.float32), precision=highest
    )
    param_map = jnp.einsum(
        "sab,sbp->sap", root_info, cont_sens[:, 0].astype(jnp.float32), precision=highest
    ).astype(jnp.bfloat16)
    cont_res = jnp.einsum("sab,sb->sa", root_info, cont_misfit[:, 0], precision=highest).astype(
        jnp.bfloat16
    )
    stacked = jnp.concatenate([weighted_sens, param_map], axis=1).reshape(-1, params)
    res_vec = jnp.concatenate([weighted_res, -cont_res], axis=1).reshape(-1)
    norm_factor = 1.0 / (sat_dev * sat_count * seg_count)
    term = lax.dot_general(
        stacked, stacked, (((0,), (0,)), ((), ())), preferred_element_type=jnp.float32
    )
    row_block = lax.psum_scatter(
        term * norm_factor, ("sat", "seg"), scatter_dimension=0, tiled=True
    )
    gram_params = lax.all_gather(row_block, "seg", axis=0, tiled=True)
    grad_term = jnp.dot(res_vec, stacked, preferred_element_type=jnp.float32) * norm_factor
    grad_params = lax.psum(grad_term, ("sat", "seg"))
    pair_gram = jnp.einsum(
        "smi,smk->sik", state_pair, state_pair, preferred_element_type=jnp.float32
    )
    pair_cross = jnp.einsum(
        "smi,smp->sip", state_pair, weighted_sens, preferred_element_type=jnp.float32
    )
    pair_grad = jnp.einsum(
        "smi,sm->si", state_pair, weighted_res, preferred_element_type=jnp.float32
    )
    map_float = param_map.astype(jnp.float32)
    res_float = cont_res.astype(jnp.float32)
    own_hess = pair_gram[:, :states, :states] + jnp.einsum(
        "sai,saj->sij", state_map, state_map, precision=highest
    )
    own_cross = pair_cross[:, :states] + jnp.einsum(
        "sai,sap->sip", state_map, map_float, precision=highest
    )
    own_grad = pair_grad[:, :states] - jnp.einsum(
        "sai,sa->si", state_map, res_float, precision=highest
    )
    next_hess = pair_gram[:, states:, states:] + jnp.einsum(
        "sai,saj->sij", root_info, root_info, precision=highest
    )
    next_cross = pair_cross[:, states:] - jnp.einsum(
        "sai,sap->sip", root_info, map_float, precision=highest
    )
    next_grad = pair_grad[:, states:] + jnp.einsum(
        "sai,sa->si", root_info, res_float, precision=highest
    )
    coupling = -jnp.einsum("sai,saj->sij", state_map, root_info, precision=highest)
    got_hess, got_cross, got_grad = passed_along((next_hess, next_cross, next_grad), "seg", 1)
    node_hess = (own_hess + got_hess)[:, None]
    node_cross = (own_cross + got_cross)[:, None]
    node_grad = (own_grad + got_grad)[:, None]
    node_coupling = coupling[:, None]
    return (gram_params, grad_params, node_hess, node_cross, node_grad, node_coupling)


def solution(mesh):
    placed = (
        P("sat", "seg", None, None),
        P("sat", "seg", None, None),
        P("sat", "seg", None),
        P("sat", "seg", None),
        P("sat", "seg"),
        P("sat", "seg", None),
        P("sat", "seg", None, None),
        P("sat", "seg", None, None),
        P("sat", "seg", None, None),
        P("sat", "seg", None),
    )
    return jax.shard_map(
        shards,
        mesh=mesh,
        in_specs=placed,
        out_specs=(
            P("sat", None),
            P(),
            P("sat", "seg", None, None),
            P("sat", "seg", None, None),
            P("sat", "seg", None),
            P("sat", "seg", None, None),
        ),
        check_vma=False,
    )
```

profile of v0, /device:TPU:16, one launch (start us, length us, event | category | flops | bytes accessed | tf_op | source)
XLA Modules:
  0.0 479.6 jit_solution(1217586959932746977)
XLA Ops:
  7.9 1.3 fusion.38
  9.2 1.3 dynamic-slice
  10.5 1.4 dynamic-update-slice
  11.9 63.0 %all-reduce = f32[32]{0:T(128)S(1)} all-reduce(f32[32]{0:T(128)S(1)} %dynamic-update-slice), channel_id=1, replica_groups=mesh['sat'=16,'seg'=32] {'seg'}, use_global_device_ids=true, to_apply=%add | all-reduce | flops 32 | bytes 256
  74.8 40.4 %while.13 = (s32[]{:T(128)}, f32[1]{0:T(128)}, s32[]{:T(128)}, f32[32,1]{0,1:T(1,128)S(1)}, s32[]{:T(128)}) while((s32[]{:T(128)}, f32[1]{0:T(128)}, s32[]{:T(128)}, f32[32,1]{0,1:T(1,128)S(1)}, s32[]{:T(128)}) %tuple.40), condition=%wide.region_2.3_spmd, body=%wide.region_1.2_spmd.sunk | while | flops 5 | bytes 115 | solution.py:19
  76.1 0.6 constant_dynamic-slice_fusion.2
  115.2 0.7 convert_reduce_fusion
  115.9 0.7 reduce.1
  116.6 0.7 reduce.3
  117.6 1.3 fusion.1
  119.2 3.3 convolution_multiply_fusion
  122.4 0.6 copy-done.5
  123.5 3.7 collective-permute-start.2
  127.6 3.1 collective-permute-start
  131.5 4.6 collective-permute-start.1
  136.5 0.9 fusion.8
  137.3 110.4 %psum.7 = f32[1024]{0:T(1024)} all-reduce(f32[1024]{0:T(1024)S(1)} %broadcast_multiply_fusion), channel_id=1, replica_groups=mesh['sat'=16,'seg'=32] {'sat','seg'}, use_global_device_ids=true, to_apply=%region_4.5 | all-reduce | flops 1024 | bytes 8192 | tf_op jit(solution)/shard_map/psum | solution.py:91
  247.8 0.7 fusion.15
  248.4 0.9 fusion.11
  249.3 1.0 fusion.6
  250.3 171.4 %all-reduce.4.cloned.1.call-done = f32[1024,1024]{1,0:T(8,128)} async-done(((f32[1024,1024]{1,0:T(8,128)}), f32[1024,1024]{1,0:T(8,128)}) %all-reduce.4.cloned.1.call-update) | async-done | bytes 4194320
  421.8 0.8 dynamic-slice_bitcast_fusion
  422.5 49.4 %all-gather = f32[32,2,1024]{2,1,0:T(2,128)S(1)} all-gather(f32[1,2,1024]{2,1,0:T(2,128)S(1)} %dynamic-slice_bitcast_fusion), channel_id=1, replica_groups=mesh['sat'=16,'seg'=32] {'seg'}, dimensions={0}, use_global_device_ids=true | all-gather | bytes 270336 | tf_op jit(solution)/shard_map/all_gather | solution.py:89
  471.9 0.9 reshape.312
  (67 shorter events, 20.7 us)
Async XLA Ops:
  7.2 111.7 %copy-start = (bf16[1,1,64,1024]{3,2,1,0:T(8,128)(2,1)S(1)}, bf16[1,1,64,1024]{3,2,1,0:T(8,128)(2,1)}, u32[]{:S(2)}) copy-start(bf16[1,1,64,1024]{3,2,1,0:T(8,128)(2,1)} %param.19) | copy-start | bytes 393220
  7.2 111.7 %copy-start.2 = (f32[1,1,64,64]{3,2,1,0:T(8,128)S(1)}, f32[1,1,64,64]{3,2,1,0:T(8,128)}, u32[]{:S(2)}) copy-start(f32[1,1,64,64]{3,2,1,0:T(8,128)} %param.20) | copy-start | bytes 49156
  7.2 414.6 %all-reduce.4.cloned.1.call-start = ((), (), s32[]{:S(2)}) async-start(), calls=%async_computation | async-start | bytes 8388608
  122.4 0.7 copy-start.5
  122.4 0.8 copy-start.3
  122.4 8.4 %copy-start.1 = (bf16[1,1,320,1024]{3,2,1,0:T(8,128)(2,1)S(1)}, bf16[1,1,320,1024]{3,2,1,0:T(8,128)(2,1)}, u32[]{:S(2)}) copy-start(bf16[1,1,320,1024]{3,2,1,0:T(8,128)(2,1)} %param.12) | copy-start | bytes 1966084
  123.5 124.3 %collective-permute-start.2 = (f32[1,64]{1,0:T(1,128)S(1)}, f32[1,64]{1,0:T(1,128)S(1)}, u32[]{:S(2)}, u32[]{:S(2)}) collective-permute-start(f32[1,64]{1,0:T(1,128)S(1)} %convolution_add_fusion), channel_id=1, source_target_pairs={{0,1},{1,2},{2,3},{3,4},{4,5},{5,6},{6,7},{7,8},{8,9},{9,10},{10,1... | collective-permute-start | bytes 776 | tf_op jit(solution)/shard_map/ppermute | solution.py:25
  127.6 8.7 %copy-start.4 = (bf16[1,1,64,64]{3,2,1,0:T(8,128)(2,1)S(1)}, bf16[1,1,64,64]{3,2,1,0:T(8,128)(2,1)}, u32[]{:S(2)}) copy-start(bf16[1,1,64,64]{3,2,1,0:T(8,128)(2,1)} %param.18) | copy-start | bytes 24580
  127.6 120.8 %collective-permute-start = (f32[1,64,64]{2,1,0:T(8,128)S(1)}, f32[1,64,64]{2,1,0:T(8,128)S(1)}, u32[]{:S(2)}, u32[]{:S(2)}) collective-permute-start(f32[1,64,64]{2,1,0:T(8,128)S(1)} %fusion.12), channel_id=1, source_target_pairs={{0,1},{1,2},{2,3},{3,4},{4,5},{5,6},{6,7},{7,8},{8,9},{9,10},{10,1... | collective-permute-start | bytes 49160 | tf_op jit(solution)/shard_map/ppermute | solution.py:25
  131.5 117.8 %collective-permute-start.1 = (f32[1,64,1024]{2,1,0:T(8,128)S(1)}, f32[1,64,1024]{2,1,0:T(8,128)S(1)}, u32[]{:S(2)}, u32[]{:S(2)}) collective-permute-start(f32[1,64,1024]{2,1,0:T(8,128)S(1)} %fusion.7), channel_id=1, source_target_pairs={{0,1},{1,2},{2,3},{3,4},{4,5},{5,6},{6,7},{7,8},{8,9},{9,10},{10,1... | collective-permute-start | bytes 786440 | tf_op jit(solution)/shard_map/ppermute | solution.py:25
Sparse Core Ops, SparseCore 0:
  122.6 299.1 all-reduce.3
where the time goes:
time: 481 us; the launch traced here: 480 us
  blocking collectives  223 us (46%)
  waiting for transfers between devices  171 us (36%)
  local copies, waits for them, and re-layouts  23.7 us (5%)
  loops' own time  21.7 us (5%)
  between operations  14.9 us (3%)
  starting transfers between devices  11.4 us (2%)
  matrix products  9.03 us (2%)
    unnamed x2, waiting for transfers between devices  171 us
    psum x1, blocking collectives, shards(): grad_params = lax.psum(grad_term, ('sat', 'seg'))  110 us
    unnamed x1, blocking collectives  63 us
    all_gather x1, blocking collectives, shards(): gram_params = lax.all_gather(row_block, 'seg', axis=0, tiled=True)  49.4 us
    another operation x1, loops' own time, entering(): return lax.fori_loop(0, devices, step, start)  21.7 us
    dynamic_slice x32, local copies, waits for them, and re-layouts, step(): new = combine(before, everything[k])  18.7 us
    ppermute x3, starting transfers between devices, passed_along(): return lax.ppermute(block, axis, route)  11.3 us
  transfers between devices with their start and end apart: 4, of which 1 were waited for; matrix products, arithmetic and copies ran while one was open for 1% of the time, Pallas kernels for 0%

commit v1 on v0

--- a/solution.py
+++ b/solution.py
@@ -88,7 +88,10 @@
     )
     gram_params = lax.all_gather(row_block, "seg", axis=0, tiled=True)
     grad_term = jnp.dot(res_vec, stacked, preferred_element_type=jnp.float32) * norm_factor
-    grad_params = lax.psum(grad_term, ("sat", "seg"))
+    find_the_boxes = lambda local_x, ax_name: jnp.sum(
+        jax.lax.all_gather(local_x, axis_name=ax_name), 0
+    )
+    grad_params = find_the_boxes(grad_term, ("sat", "seg"))
     pair_gram = jnp.einsum(
         "smi,smk->sik", state_pair, state_pair, preferred_element_type=jnp.float32
     )

time: 481 us -> 551 us (1.15)
  the two profiles are of different devices: /device:TPU:16 before, /device:TPU:1 now
where the time goes in v1:
time: 551 us; the launch traced here: 550 us
  waiting for transfers between devices  369 us (67%)
  blocking collectives  99.3 us (18%)
  local copies, waits for them, and re-layouts  25.3 us (5%)
  loops' own time  21.7 us (4%)
  between operations  14.9 us (3%)
  matrix products  9.03 us (2%)
  other arithmetic  6.05 us (1%)
    unnamed x3, waiting for transfers between devices  290 us
    all_gather x1, waiting for transfers between devices, shards(): jax.lax.all_gather(local_x, axis_name=ax_name)  78.8 us
    unnamed x1, blocking collectives  61.9 us
    all_gather x1, blocking collectives, shards(): gram_params = lax.all_gather(row_block, 'seg', axis=0, tiled=True)  37.4 us
    another operation x1, loops' own time, entering(): return lax.fori_loop(0, devices, step, start)  21.7 us
    dynamic_slice x32, local copies, waits for them, and re-layouts, step(): new = combine(before, everything[k])  18.7 us
  transfers between devices with their start and end apart: 5, of which 3 were waited for; matrix products, arithmetic and copies ran while one was open for 1% of the time, Pallas kernels for 0%

profile of v1, /device:TPU:1, one launch (start us, length us, event | category | flops | bytes accessed | tf_op | source)
XLA Modules:
  0.0 549.8 jit_solution(7295292255298978156)
XLA Ops:
  7.9 1.3 fusion.38
  9.2 1.3 dynamic-slice
  10.5 1.4 dynamic-update-slice
  11.9 61.9 %all-reduce = f32[32]{0:T(128)S(1)} all-reduce(f32[32]{0:T(128)S(1)} %dynamic-update-slice), channel_id=1, replica_groups=mesh['sat'=16,'seg'=32] {'seg'}, use_global_device_ids=true, to_apply=%add | all-reduce | flops 32 | bytes 256
  73.8 40.4 %while.13 = (s32[]{:T(128)}, f32[1]{0:T(128)}, s32[]{:T(128)}, f32[32,1]{0,1:T(1,128)S(1)}, s32[]{:T(128)}) while((s32[]{:T(128)}, f32[1]{0:T(128)}, s32[]{:T(128)}, f32[32,1]{0,1:T(1,128)S(1)}, s32[]{:T(128)}) %tuple.42), condition=%wide.region_2.3_spmd, body=%wide.region_1.2_spmd.sunk | while | flops 5 | bytes 115 | solution.py:19
  114.2 0.7 convert_reduce_fusion
  114.9 0.7 reduce.1
  115.6 0.7 reduce.3
  116.5 1.3 fusion.1
  118.1 3.3 convolution_multiply_fusion
  123.3 1.3 collective-permute-start.2
  125.1 1.3 collective-permute-start
  127.2 1.3 collective-permute-start.1
  128.7 0.9 fusion.8
  130.2 0.9 fusion.11
  131.0 0.8 collective-permute-done.1
  131.8 1.0 fusion.6
  132.8 289.9 %all-reduce.4.cloned.1.call-done = f32[1024,1024]{1,0:T(8,128)} async-done(((f32[1024,1024]{1,0:T(8,128)}), f32[1024,1024]{1,0:T(8,128)}) %all-reduce.4.cloned.1.call-update) | async-done | bytes 4194320
  422.7 0.8 dynamic-slice_bitcast_fusion
  423.4 37.4 %all-gather.1 = f32[32,2,1024]{2,1,0:T(2,128)S(1)} all-gather(f32[1,2,1024]{2,1,0:T(2,128)S(1)} %dynamic-slice_bitcast_fusion), channel_id=1, replica_groups=mesh['sat'=16,'seg'=32] {'seg'}, dimensions={0}, use_global_device_ids=true | all-gather | bytes 270336 | tf_op jit(solution)/shard_map/all_gather | solution.py:89
  460.8 0.9 reshape.313
  461.7 78.8 %all-gather.4.cloned.1.call-done = f32[524288]{0:T(1024)} async-done(((f32[1024]{0:T(1024)}), f32[524288]{0:T(1024)}) %all-gather.4.cloned.1.call-update) | async-done | bytes 2097168 | tf_op jit(solution)/shard_map/all_gather | solution.py:92
  540.5 1.7 reshape.308
  542.2 0.7 reduce_sum.19
  (71 shorter events, 23.1 us)
Async XLA Ops:
  7.2 110.6 %copy-start = (bf16[1,1,64,1024]{3,2,1,0:T(8,128)(2,1)S(1)}, bf16[1,1,64,1024]{3,2,1,0:T(8,128)(2,1)}, u32[]{:S(2)}) copy-start(bf16[1,1,64,1024]{3,2,1,0:T(8,128)(2,1)} %param.19) | copy-start | bytes 393220
  7.2 110.6 %copy-start.2 = (f32[1,1,64,64]{3,2,1,0:T(8,128)S(1)}, f32[1,1,64,64]{3,2,1,0:T(8,128)}, u32[]{:S(2)}) copy-start(f32[1,1,64,64]{3,2,1,0:T(8,128)} %param.20) | copy-start | bytes 49156
  7.2 415.5 %all-reduce.4.cloned.1.call-start = ((), (), s32[]{:S(2)}) async-start(), calls=%async_computation.1 | async-start | bytes 8388608
  121.3 0.7 copy-start.5
  121.3 1.7 copy-start.3
  121.4 5.1 copy-start.1
  121.4 419.1 %all-gather.4.cloned.1.call-start = ((), (), s32[]{:S(2)}) async-start(), calls=%async_computation | async-start | bytes 2101248 | tf_op jit(solution)/shard_map/all_gather | solution.py:92
  122.4 6.1 %copy-start.4 = (bf16[1,1,64,64]{3,2,1,0:T(8,128)(2,1)S(1)}, bf16[1,1,64,64]{3,2,1,0:T(8,128)(2,1)}, u32[]{:S(2)}) copy-start(bf16[1,1,64,64]{3,2,1,0:T(8,128)(2,1)} %param.18) | copy-start | bytes 24580
  123.3 6.2 %collective-permute-start.2 = (f32[1,64]{1,0:T(1,128)S(1)}, f32[1,64]{1,0:T(1,128)S(1)}, u32[]{:S(2)}, u32[]{:S(2)}) collective-permute-start(f32[1,64]{1,0:T(1,128)S(1)} %convolution_add_fusion), channel_id=1, source_target_pairs={{0,1},{1,2},{2,3},{3,4},{4,5},{5,6},{6,7},{7,8},{8,9},{9,10},{10,1... | collective-permute-start | bytes 776 | tf_op jit(solution)/shard_map/ppermute | solution.py:25
  125.1 5.0 collective-permute-start
  127.2 4.6 collective-permute-start.1
Sparse Core Ops, SparseCore 0:
  121.5 301.1 all-reduce.3
  427.4 113.0 all-gather.3
